TPU v7x, 256 devices: a whole 4x4x8 slice. The times are simulated.
256 devices in a mesh: band: 8 (over y, core), slab: 32 (over z, x).
Axes of the slice: x: 4, y: 4, z: 8, core: 2. Of those that a mesh axis runs over, the one named last changes fastest.
Arguments:
- bands: float32 [2, 256, 131072], P(None, ('band', 'slab')), may hold values from -6 to 6
- projectors: float32 [16384, 512], P('slab'), may hold values from -0.625 to 0.625
- slot_atom: int32 [16384], P('slab'), may hold values from -1 to 3071, as said below
- slot_box: int32 [16384], P('slab'), may hold values from 0 to 63
- channels: int32 [3072], replicated, may hold values from 1 to 8
- coupling: float32 [8, 8, 3072], replicated, may hold values from -2 to 2
Outputs:
- applied: float32 [2, 256, 131072], P(None, ('band', 'slab'))
Inputs may be any that keep to these rules, and one draw needn't show every extreme that they name: `slot_atom`: atom a is owned by slab a // 96. A live slot k names an atom owned by slab k // 512 or by the slab before it, cyclically. In each slab's 512 slots the live ones come first; some slab has all of its slots live.
All inputs are finite; a program needn't handle non-finite values.
Results may differ from a plain program's by a relative error of at most 0.0003.
Values sent between devices are 32-bit elements; how exact they have to be, the bound alone decides.
A program may use at most 128 MiB of HBM per device.

v0:
```python
import jax
import jax.numpy as jnp
from jax import lax
from jax.sharding import PartitionSpec as P

BOXPTS = 64


def passed_along(block, axis, distance):
    devices = range(lax.axis_size(axis))
    route = [((i - distance) % len(devices), i) for i in devices]
    return lax.ppermute(block, axis, route)


def couple(partial_value, coupling_rows, mask_rows, channel):
    nitems, atom_rows, width = partial_value.shape
    shaped = (
        partial_value.reshape(nitems, atom_rows, channel, width // channel)
        * mask_rows[None, :, :, None]
    )
    mixed = jnp.einsum("cea,naeb->nacb", coupling_rows, shaped, precision=lax.Precision.HIGHEST)
    return (mixed * mask_rows[None, :, :, None]).reshape(nitems, atom_rows, width)


def body(bands, projectors, slot_atom, slot_box, channels, coupling):
    nblock, band_local, ngrid = bands.shape
    highest = lax.Precision.HIGHEST
    nslab = lax.axis_size("slab")
    slab_index = lax.axis_index("slab")
    natoms = channels.shape[0]
    atom_dev = natoms // nslab
    channel = coupling.shape[0]
    slots = slot_atom.shape[0]
    boxes = ngrid // (nslab * BOXPTS)
    beta = projectors.reshape(slots, channel, BOXPTS)
    prev_start = (slab_index - 1) % nslab * atom_dev
    own_start = slab_index * atom_dev
    relative = (slot_atom - prev_start) % natoms
    columns = jnp.arange(2 * atom_dev, dtype=jnp.int32)
    selector = ((relative[:, None] == columns[None, :]) & (slot_atom[:, None] >= 0)).astype(
        jnp.float32
    )
    count_rows = jnp.concatenate(
        [
            lax.dynamic_slice_in_dim(channels, prev_start, atom_dev),
            lax.dynamic_slice_in_dim(channels, own_start, atom_dev),
        ]
    )
    mask_rows = (jnp.arange(channel, dtype=jnp.int32)[None, :] < count_rows[:, None]).astype(
        jnp.float32
    )
    coupling_rows = jnp.concatenate(
        [
            lax.dynamic_slice_in_dim(coupling, prev_start, atom_dev, 2),
            lax.dynamic_slice_in_dim(coupling, own_start, atom_dev, 2),
        ],
        axis=2,
    )
    arranged = bands.reshape(nblock, band_local, nslab, boxes * BOXPTS)
    arrived = lax.all_to_all(arranged, "slab", split_axis=2, concat_axis=1, tiled=True)
    nitems = arrived.shape[0]
    gathered_bands = arrived.shape[1]
    width = channel * gathered_bands
    slab_grid = arrived.reshape(nitems, gathered_bands, boxes, BOXPTS).transpose(0, 2, 1, 3)
    slab_grid = slab_grid.reshape(nitems, boxes, gathered_bands * BOXPTS)
    patches = jnp.take(slab_grid, slot_box, axis=1).reshape(nitems, slots, gathered_bands, BOXPTS)
    projected = jnp.einsum("nkbg,kcg->nkcb", patches, beta, precision=highest).reshape(
        nitems, slots, width
    )
    partial_value = jnp.einsum("ka,nkx->nax", selector, projected, precision=highest)
    upper = passed_along(partial_value[:, :atom_dev], "slab", -1)
    own_total = partial_value[:, atom_dev:] + upper
    own_coef = couple(own_total, coupling_rows[:, :, atom_dev:], mask_rows[atom_dev:], channel)
    lower_coef = passed_along(own_coef, "slab", 1)
    coef = jnp.concatenate([lower_coef, own_coef], axis=1)
    per_slot = jnp.einsum("ka,nax->nkx", selector, coef, precision=highest)
    per_slot = per_slot.reshape(nitems, slots, channel, gathered_bands)
    contrib = jnp.einsum("nkcb,kcg->nkbg", per_slot, beta, precision=highest)
    contrib = contrib.reshape(nitems, slots, gathered_bands * BOXPTS)
    summed = (
        jnp.zeros((nitems, boxes, gathered_bands * BOXPTS), jnp.float32)
        .at[:, slot_box, :]
        .add(contrib)
    )
    returning = summed.reshape(nitems, boxes, gathered_bands, BOXPTS).transpose(0, 2, 1, 3)
    returning = returning.reshape(nitems, gathered_bands, 1, boxes * BOXPTS)
    result = lax.all_to_all(returning, "slab", split_axis=1, concat_axis=2, tiled=True)
    return result.reshape(nblock, band_local, ngrid)


def solution(mesh):
    in_specs = (P(None, ("band", "slab"), None), P("slab", None), P("slab"), P("slab"), P(), P())
    out_specs = P(None, ("band", "slab"), None)
    return jax.shard_map(body, mesh=mesh, in_specs=in_specs, out_specs=out_specs, check_vma=False)
```

profile of v0, /device:TPU:8, one launch (start us, length us, event | category | flops | bytes accessed | tf_op | source)
XLA Modules:
  0.0 368.9 jit_solution(8380382376638940725)
XLA Ops:
  0.0 5.2 %reduce = f32[2,131072]{1,0:T(2,128)} reduce(f32[2,1,131072]{2,1,0:T(1,128)} %param.6, f32[]{:T(128)} %constant.55), dimensions={1}, to_apply=%param.6.reduce_sub_computation | reduce | bytes 2097156 | tf_op args[0]
  5.3 11.5 %all-to-all-start = ((f32[2,1,32,4096]{3,0,1,2:T(2,128)}), f32[2,1,32,4096]{3,0,1,2:T(2,128)S(1)}, u32[]{:S(2)}, u32[]{:S(2)}) async-start(f32[2,1,32,4096]{3,0,1,2:T(2,128)} %bitcast.26), calls=%async_computation | async-start | bytes 2097152 | tf_op jit(solution)/shard_map/all_to_all | solution.py:60
  16.8 1.6 copy.81
  18.3 2.0 copy.100
  20.3 0.8 fusion.16
  21.1 0.1 pad_add_fusion
  21.2 0.1 slice.20
  21.3 0.5 copy-done.4
  21.9 22.9 %all-to-all-done = f32[2,1,32,4096]{3,0,1,2:T(2,128)S(1)} async-done(((f32[2,1,32,4096]{3,0,1,2:T(2,128)}), f32[2,1,32,4096]{3,0,1,2:T(2,128)S(1)}, u32[]{:S(2)}, u32[]{:S(2)}) %all-to-all-start) | async-done | bytes 1048608 | tf_op jit(solution)/shard_map/all_to_all | solution.py:60
  44.8 1.6 copy.77
  46.4 2.0 reshape.57
  48.4 2.6 copy.104
  50.9 2.4 reshape.90
  53.4 19.3 %gather_fusion = f32[512,2,2048]{2,1,0:T(2,128)} fusion(f32[2,64,2048]{2,0,1:T(2,128)S(1)} %reshape.90, s32[1024]{0:T(1024)S(1)} %pad_clamp_fusion), kind=kCustom, calls=%fused_computation | custom fusion | bytes 16779264 | tf_op jit(solution)/shard_map/jit(_take)/gather | solution.py:66
  72.7 13.2 %copy.80 = f32[2,512,2048]{1,2,0:T(8,128)} copy(f32[2,512,2048]{2,0,1:T(2,128)} %bitcast.58) | data formatting | bytes 16777216 | tf_op jit(solution)/shard_map/jit(_take)/gather | solution.py:66
  85.9 8.5 %broadcast_select_fusion = f32[2,512,32,64]{1,3,2,0:T(8,128)} fusion(f32[2,512,32,64]{1,3,2,0:T(8,128)} %bitcast.57, pred[512]{0:T(512)(128)(4,1)S(1)} %compare_and_fusion), kind=kLoop, calls=%fused_computation.3 | loop fusion | flops 2097152 | bytes 16777728 | tf_op jit(solution)/shard_map/jit(_take)/select_n | solution.py:66
  94.4 16.4 %copy.82 = f32[2,512,32,64]{3,2,0,1:T(8,128)} copy(f32[2,512,32,64]{1,3,2,0:T(8,128)} %broadcast_select_fusion) | data formatting | bytes 16777216 | tf_op jit(solution)/shard_map/jit(_take)/select_n | solution.py:66
  110.8 69.3 %convolution_bitcast_fusion.1 = f32[2,512,8,32]{3,2,0,1:T(8,128)} fusion(f32[2,512,32,64]{3,2,0,1:T(8,128)} %copy.82, f32[512,8,64,1]{2,1,3,0:T(8,128)S(1)} %copy-done.2), kind=kOutput, calls=%fused_computation.4 | convolution fusion | flops 201326592 | bytes 10485760 | tf_op jit(solution)/shard_map/nkbg,kcg->nkcb/dot_general | solution.py:67
  180.1 3.8 %copy.84 = f32[2,512,8,32]{1,3,2,0:T(8,128)} copy(f32[2,512,8,32]{3,2,0,1:T(8,128)} %convolution_bitcast_fusion.1) | data formatting | bytes 2097152 | tf_op jit(solution)/shard_map/nkbg,kcg->nkcb/transpose | solution.py:67
  183.9 2.0 convolution_bitcast_fusion.2
  185.9 1.5 collective-permute-start
  187.4 0.1 fusion.14
  187.5 0.7 copy.87
  188.1 0.1 constant_dynamic-slice_fusion
  188.2 0.9 copy.110
  189.1 2.6 collective-permute-done
  191.7 1.0 slice_add_fusion
  192.7 0.1 copy.86
  192.8 0.7 broadcast_multiply_fusion
  193.5 0.4 copy.89
  193.9 2.7 fusion
  196.6 1.4 copy.90
  198.1 0.1 copy.91
  198.2 1.9 collective-permute-start.1
  200.1 7.2 %collective-permute-done.1 = f32[2,96,256]{2,1,0:T(8,128)S(1)} collective-permute-done((f32[2,96,256]{2,1,0:T(8,128)S(1)}, f32[2,96,256]{2,1,0:T(8,128)S(1)}, u32[]{:S(2)}, u32[]{:S(2)}) %collective-permute-start.1) | collective-permute-done | bytes 196640 | tf_op jit(solution)/shard_map/ppermute | solution.py:12
  207.3 2.3 fusion.1
  209.5 4.6 %copy.93 = f32[2,512,8,32]{3,2,0,1:T(8,128)} copy(f32[2,512,8,32]{1,3,2,0:T(8,128)} %bitcast.61) | data formatting | bytes 2097152 | tf_op jit(solution)/shard_map/reshape | solution.py:77
  214.1 30.1 %convolution_bitcast_fusion = f32[2,512,32,64]{3,2,0,1:T(8,128)} fusion(f32[2,512,8,32]{3,2,0,1:T(8,128)} %copy.93, f32[512,8,64,1]{2,1,3,0:T(8,128)S(1)} %copy-done.2), kind=kOutput, calls=%fused_computation.2 | convolution fusion | flops 201326592 | bytes 10485760 | tf_op jit(solution)/shard_map/nkcb,kcg->nkbg/dot_general | solution.py:78
  244.2 12.8 %copy.95 = f32[2,512,32,64]{1,3,2,0:T(8,128)} copy(f32[2,512,32,64]{3,2,0,1:T(8,128)} %convolution_bitcast_fusion) | data formatting | bytes 16777216 | tf_op jit(solution)/shard_map/nkcb,kcg->nkbg/transpose | solution.py:78
  257.0 13.4 %copy.96 = f32[512,2,2048]{2,1,0:T(2,128)} copy(f32[512,2,2048]{0,2,1:T(8,128)} %bitcast.56) | data formatting | bytes 16777216 | tf_op jit(solution)/shard_map/reshape | solution.py:79
  270.4 0.5 broadcast_in_dim.14
  270.9 56.4 %scatter_fusion = f32[2,64,2048]{2,0,1:T(2,128)S(1)} fusion(f32[2,64,2048]{2,0,1:T(2,128)S(1)} %broadcast_in_dim.14, s32[512]{0:T(512)S(1)} %copy-done.5, f32[512,2,2048]{2,1,0:T(2,128)} %copy.96), kind=kCustom, calls=%fused_computation.1 | custom fusion | flops 2097152 | bytes 25167872 | tf_op jit(solution)/shard_map/scatter-add | solution.py:83
  327.3 2.5 reshape.65
  329.8 2.8 copy.112
  332.6 1.6 reshape.66
  334.3 2.0 copy.98
  336.3 30.3 %all_to_all.8 = f32[2,32,1,4096]{3,0,2,1:T(2,128)S(1)} all-to-all(f32[2,32,1,4096]{3,0,2,1:T(2,128)S(1)} %copy.98), channel_id=1, replica_groups=mesh['band'=8,'slab'=32] {'slab'}, dimensions={1} | all-to-all | bytes 2097152 | tf_op jit(solution)/shard_map/all_to_all | solution.py:87
  366.6 2.0 copy.99
  (23 shorter events, 0.1 us)
Async XLA Ops:
  0.0 188.1 %copy-start = (f32[8,8,3072]{2,1,0:T(8,128)S(1)}, f32[8,8,3072]{2,1,0:T(8,128)}, u32[]{:S(2)}) copy-start(f32[8,8,3072]{2,1,0:T(8,128)} %param.11) | copy-start | bytes 2359300
  0.0 21.3 %copy-start.6 = (s32[512]{0:T(512)S(1)}, s32[512]{0:T(512)}, u32[]{:S(2)}) copy-start(s32[512]{0:T(512)} %param.9) | copy-start | bytes 6148
  0.0 21.3 %copy-start.7 = (s32[512]{0:T(512)S(1)}, s32[512]{0:T(512)}, u32[]{:S(2)}) copy-start(s32[512]{0:T(512)} %param.8) | copy-start | bytes 6148
  5.3 39.5 %all-to-all-start = ((f32[2,1,32,4096]{3,0,1,2:T(2,128)}), f32[2,1,32,4096]{3,0,1,2:T(2,128)S(1)}, u32[]{:S(2)}, u32[]{:S(2)}) async-start(f32[2,1,32,4096]{3,0,1,2:T(2,128)} %bitcast.26), calls=%async_computation | async-start | bytes 2097152 | tf_op jit(solution)/shard_map/all_to_all | solution.py:60
  21.3 0.6 copy-start.4
  21.9 162.0 %copy-start.8 = (pred[512]{0:T(512)(128)(4,1)}, pred[512]{0:T(512)(128)(4,1)S(1)}, u32[]{:S(2)}) copy-start(pred[512]{0:T(512)(128)(4,1)S(1)} %broadcast_compare_fusion) | copy-start | bytes 1540
  21.9 162.0 %copy-start.3 = (s32[512]{0:T(512)}, s32[512]{0:T(512)S(1)}, u32[]{:S(2)}) copy-start(s32[512]{0:T(512)S(1)} %add_select_fusion) | copy-start | bytes 6148
  94.4 16.4 %copy-start.2 = (f32[512,8,64,1]{2,1,3,0:T(8,128)S(1)}, f32[512,8,64,1]{2,1,3,0:T(8,128)}, u32[]{:S(2)}) copy-start(f32[512,8,64,1]{2,1,3,0:T(8,128)} %copy.100) | copy-start | bytes 3145732
  185.9 5.9 %collective-permute-start = (f32[2,96,256]{2,1,0:T(8,128)S(1)}, f32[2,96,256]{2,1,0:T(8,128)}, u32[]{:S(2)}, u32[]{:S(2)}) collective-permute-start(f32[2,96,256]{2,1,0:T(8,128)S(1)} %slice.19), channel_id=1, source_target_pairs={{1,0},{2,1},{3,2},{4,3},{5,4},{6,5},{7,6},{8,7},{9,8},{10,9},{11,1... | collective-permute-start | bytes 589832 | tf_op jit(solution)/shard_map/ppermute | solution.py:12
  198.2 9.1 %collective-permute-start.1 = (f32[2,96,256]{2,1,0:T(8,128)S(1)}, f32[2,96,256]{2,1,0:T(8,128)S(1)}, u32[]{:S(2)}, u32[]{:S(2)}) collective-permute-start(f32[2,96,256]{2,1,0:T(8,128)S(1)} %copy.91), channel_id=1, source_target_pairs={{31,0},{0,1},{1,2},{2,3},{3,4},{4,5},{5,6},{6,7},{7,8},{8,9},{9,10... | collective-permute-start | bytes 589832 | tf_op jit(solution)/shard_map/ppermute | solution.py:12
  257.0 13.9 %copy-start.5 = (s32[512]{0:T(512)S(1)}, s32[512]{0:T(512)}, u32[]{:S(2)}) copy-start(s32[512]{0:T(512)} %copy-done.4) | copy-start | bytes 6148
  270.9 97.8 %copy-start.1 = (f32[8,8,3072]{2,1,0:T(8,128)S(1)}, f32[8,8,3072]{2,1,0:T(8,128)}, u32[]{:S(2)}) copy-start(f32[8,8,3072]{2,1,0:T(8,128)} %param.11) | copy-start | bytes 2359300
where the time goes:
time: 375 us; the launch traced here: 369 us
  local copies, waits for them, and re-layouts  112 us (30%)
  matrix products  106 us (28%)
  other arithmetic  72 us (19%)
  waiting for transfers between devices  32.7 us (9%)
  blocking collectives  30.3 us (8%)
  starting transfers between devices  14.9 us (4%)
    dot_general x1, matrix products, body(): jnp.einsum('nkbg,kcg->nkcb', patches, beta, precision=highest)  69.3 us
    scatter-add x1, other arithmetic, body(): summed = jnp.zeros((nitems, boxes, gathered_bands * BOXPTS), jnp.float32)...  56.4 us
    gather x2, local copies, waits for them, and re-layouts, body(): jnp.take(slab_grid, slot_box, axis=1)  32.5 us
    all_to_all x1, blocking collectives, body(): lax.all_to_all(returning, 'slab', split_axis=1, concat_axis=2, tiled=True)  30.3 us
    dot_general x1, matrix products, body(): contrib = jnp.einsum('nkcb,kcg->nkbg', per_slot, beta, precision=highest)  30.1 us
    all_to_all x1, waiting for transfers between devices, body(): lax.all_to_all(arranged, 'slab', split_axis=2, concat_axis=1, tiled=True)  22.9 us
    select_n x1, local copies, waits for them, and re-layouts, body(): jnp.take(slab_grid, slot_box, axis=1)  16.4 us
    reshape x1, local copies, waits for them, and re-layouts, body(): contrib = contrib.reshape(nitems, slots, gathered_bands * BOXPTS)  13.4 us
  transfers between devices with their start and end apart: 3, of which 3 were waited for; matrix products, arithmetic and copies ran while one was open for 2% of the time, Pallas kernels for 0%

commit v1 on v0

v1 whole, which is shorter than its diff:
```python
import jax
import jax.numpy as jnp
from jax import lax
from jax.experimental import pallas as pl
from jax.experimental.pallas import tpu as pltpu
from jax.sharding import PartitionSpec as P

MESH = pl.DeviceIdType.MESH
F32 = jnp.float32
BF16 = jnp.bfloat16
NSLAB = 32
PTS = 64
BOXES = 64
TILES = BOXES // 2
SLOTS = 512
HALF = SLOTS // 2
CH = 8
ATOMS = 96
NATOM = NSLAB * ATOMS
NB = 32
WIN = 256


def split(x):
    hi = x.astype(BF16)
    lo = (x - hi.astype(F32)).astype(BF16)
    return hi, lo


def mm(a, b):
    return jnp.dot(a, b, preferred_element_type=F32)


def mm_nt(a, b, precision=None):
    return lax.dot_general(
        a, b, (((1,), (1,)), ((), ())), preferred_element_type=F32, precision=precision
    )


def iota(shape, axis):
    return lax.broadcasted_iota(jnp.int32, shape, axis)


def prepare_slots(pj, lf, lhs, bw):
    for q in range(4):
        v = pj[:, 128 * q : 128 * (q + 1)]
        lf[pl.ds(2 * q, SLOTS, stride=CH), :] = v
        lf[pl.ds(2 * q + 1, SLOTS, stride=CH), :] = pltpu.roll(v, 64, 1)
    low = iota((128, 128), 1) < 64

    def one(i, carry):
        rows = pl.ds(pl.multiple_of(i * 128, 128), 128)
        x = lf[rows, :]
        both = jnp.where(low, x, pltpu.roll(x, 64, 1))
        hi = both.astype(BF16).astype(F32)
        lo = both - hi
        lhs[rows, 0:128] = hi.astype(BF16)
        lhs[rows, 128:256] = jnp.where(low, lo, 0.0).astype(BF16)
        lf[rows, :] = both
        return carry

    lax.fori_loop(0, SLOTS * CH // 128, one, 0)
    keep = (iota((16, 128), 0) < 8) == (iota((16, 128), 1) < 64)

    def two(g, carry):
        for i in range(8):
            first = pl.multiple_of((g * 8 + i) * CH, CH)
            second = pl.multiple_of((HALF + g * 8 + i) * CH, CH)
            x = jnp.concatenate([lf[pl.ds(first, CH), :], lf[pl.ds(second, CH), :]], axis=0)
            x = jnp.where(keep, x, 0.0)
            hi = x.astype(BF16)
            lo = (x - hi.astype(F32)).astype(BF16)
            bw[g, 16 * i : 16 * (i + 1), 0:128] = hi
            bw[g, 16 * i : 16 * (i + 1), 128:256] = lo
        return carry

    lax.fori_loop(0, HALF // 8, two, 0)


def prepare_tables(me, meta, cw, sel, b4, md, start):
    slot_atom = meta[0:1, 0:SLOTS]
    slot_box = meta[0:1, SLOTS : 2 * SLOTS]
    live = slot_atom >= 0
    prev_start = lax.rem(me + NSLAB - 1, NSLAB) * ATOMS
    rel = slot_atom - prev_start
    rel = jnp.where(rel < 0, rel + NATOM, rel)
    rel = jnp.where(live, rel, -1)
    sel[...] = jnp.where(iota((2 * ATOMS, SLOTS), 0) == rel, 1.0, 0.0).astype(BF16)
    box = jnp.where(live, slot_box, -1)
    row = iota((TILES, HALF), 0)
    for i2 in range(2):
        part = box[:, HALF * i2 : HALF * (i2 + 1)]
        for p in range(2):
            at = (2 * i2 + p) * TILES
            b4[at : at + TILES, :] = jnp.where(2 * row + p == part, 1.0, 0.0).astype(BF16)
    offset = me * ATOMS - start
    own = jnp.where(iota((ATOMS, WIN), 1) == iota((ATOMS, WIN), 0) + offset, 1.0, 0.0)
    mixing = mm_nt(own, cw[0:72, :], lax.Precision.HIGHEST)
    count = mixing[:, 64:65]
    pair_channel = iota((ATOMS, 64), 1)
    keep = (lax.div(pair_channel, CH).astype(F32) < count) & (
        lax.rem(pair_channel, CH).astype(F32) < count
    )
    mixing = jnp.where(keep, mixing[:, 0:64], 0.0)
    pair = iota((64, CH * NB), 0)
    to = lax.div(iota((64, CH * NB), 1), NB)
    for d in range(CH):
        source = lax.rem(to + CH - d, CH)
        spread = jnp.where(pair == to * CH + source, 1.0, 0.0)
        md[d] = jnp.dot(
            mixing, spread, preferred_element_type=F32, precision=lax.Precision.HIGHEST
        )


def split_bands(xb, xs):
    low = iota((NB, 128), 1) < 64

    def one(r, carry):
        x = xb[r]
        turned = pltpu.roll(x, 64, 1)
        for p in range(2):
            both = jnp.where(low, x, turned) if p == 0 else jnp.where(low, turned, x)
            hi = both.astype(BF16).astype(F32)
            lo = both - hi
            xs[2 * r + p, :, 0:128] = jnp.where(low, hi, lo).astype(BF16)
            xs[2 * r + p, :, 128:256] = hi.astype(BF16)
        return carry

    lax.fori_loop(0, TILES, one, 0, unroll=2)


def project(slot_box, lhs, xs, pc, sel, q):
    def one(g, carry):
        base = g * 8
        weights = jnp.concatenate([xs[slot_box[base + i]] for i in range(8)], axis=0)
        rows = pl.ds(pl.multiple_of(base * CH, 64), 64)
        out = mm_nt(lhs[rows, :], weights)
        for i in range(8):
            tile = out[8 * i : 8 * i + 8, 128 * (i // 4) : 128 * (i // 4 + 1)]
            if i % 4:
                tile = pltpu.roll(tile, 128 - NB * (i % 4), 1)
            pc[pl.ds(base + i, CH, stride=SLOTS), :] = tile
        return carry

    lax.fori_loop(0, SLOTS // 8, one, 0, unroll=4)
    values = jnp.concatenate(
        [pc[SLOTS * c : SLOTS * (c + 1), 0:NB] for c in range(CH)], axis=1
    )
    hi, lo = split(values)
    q[...] = mm(sel[...], hi) + mm(sel[...], lo)


def couple(q, up, md, cf):
    total = q[ATOMS : 2 * ATOMS, :] + up[...]
    mixed = md[0] * total
    for d in range(1, CH):
        mixed = mixed + md[d] * pltpu.roll(total, NB * d, 1)
    cf[ATOMS : 2 * ATOMS, :] = mixed


def contribute(me, slot_atom, cf, k3, bw, cc):
    for c in range(CH):
        tile = cf[:, 128 * (c // 4) : 128 * (c // 4 + 1)]
        if c % 4:
            tile = pltpu.roll(tile, 128 - NB * (c % 4), 1)
        k3[:, c, :] = tile
    prev_start = lax.rem(me + NSLAB - 1, NSLAB) * ATOMS
    pair_of = lax.div(lax.rem(iota((NB, WIN), 1), 128), 16)

    def coefficients(k):
        atom = slot_atom[k]
        rel = atom - prev_start
        rel = jnp.where(rel < 0, rel + NATOM, rel)
        rel = jnp.where((atom < 0) | (rel >= 2 * ATOMS), 0, rel)
        return k3[rel]

    def one(g, carry):
        parts = []
        for i in range(8):
            parts.append(coefficients(g * 8 + i))
            parts.append(coefficients(HALF + g * 8 + i))
        turned = jnp.transpose(jnp.concatenate(parts, axis=0))[0:NB, :]
        hi = turned.astype(BF16).astype(F32)
        lo = turned - hi
        both = jnp.concatenate([hi, lo], axis=1)
        rows = jnp.concatenate(
            [jnp.where(pair_of == i, both, 0.0).astype(BF16) for i in range(8)], axis=0
        )
        weights = bw[g]
        out = mm(rows, jnp.concatenate([weights, weights], axis=0))
        cc[pl.ds(pl.multiple_of(g * 256, 256), 256), :] = out[:, 0:128] + out[:, 128:256]
        return carry

    lax.fori_loop(0, HALF // 8, one, 0, unroll=2)


def gather_boxes(n, cc, b4, y):
    low = iota((TILES, 128), 1) < 64
    hi, lo = split(cc[pl.ds(n, HALF, stride=NB), :])
    out = mm(b4[...], jnp.concatenate([hi, lo], axis=1))
    out = out[:, 0:128] + out[:, 128:256]
    stay = jnp.where(low, out[0:32], out[96:128])
    move = jnp.where(low, out[32:64], out[64:96])
    y[n] = stay + pltpu.roll(move, 64, 1)


def kernel(
    slot_atom, slot_box, meta, bands, projectors, coupling,
    out,
    xb, xs, pj, lf, lhs, bw, sel, b4, md, cw, pc, q, up, cf, k3, cc, y,
    in_send, in_recv, out_send, out_recv, up_send, up_recv, low_send, low_recv, load_sem, self_sem,
):
    me = lax.axis_index("slab")
    after = lax.rem(me + 1, NSLAB)
    before = lax.rem(me + NSLAB - 1, NSLAB)
    start = pl.multiple_of(jnp.minimum(lax.div(me * ATOMS, 128) * 128, NATOM - WIN), 128)
    load_slots = pltpu.make_async_copy(projectors, pj, load_sem.at[0])
    load_slots.start()
    load_mix = pltpu.make_async_copy(
        coupling.at[:, pl.ds(start, WIN)], cw.at[0:64, :], load_sem.at[1]
    )
    load_mix.start()

    barrier = pltpu.get_barrier_semaphore()

    def greet(i, carry):
        pl.semaphore_signal(
            barrier, inc=1, device_id={"slab": lax.rem(me + i, NSLAB)}, device_id_type=MESH
        )
        return carry

    lax.fori_loop(1, NSLAB, greet, 0)
    pl.semaphore_wait(barrier, NSLAB - 1)

    def rows_of(slab):
        return pl.ds(pl.multiple_of(slab * TILES, TILES), TILES)

    def self_in(blk):
        return pltpu.make_async_copy(
            bands.at[blk, rows_of(me), :], xb.at[blk, :, me, :], self_sem.at[blk]
        )

    def self_out(blk):
        return pltpu.make_async_copy(
            y.at[blk, me], out.at[blk, rows_of(me), :], self_sem.at[2 + blk]
        )

    def remote(src, dst, send_sem, recv_sem, peer):
        return pltpu.make_async_remote_copy(
            src, dst, send_sem, recv_sem, device_id={"slab": peer}, device_id_type=MESH
        )

    for blk in range(2):

        def send(i, carry):
            peer = lax.rem(me + i, NSLAB)
            remote(
                bands.at[blk, rows_of(peer), :],
                xb.at[blk, :, me, :],
                in_send.at[blk],
                in_recv.at[blk],
                peer,
            ).start()
            return carry

        lax.fori_loop(1, NSLAB, send, 0)
        self_in(blk).start()

    def whole(ref, sem):
        part = ref.at[0 : NSLAB - 1]
        return pltpu.make_async_copy(part, part, sem)

    def up_copy(blk):
        return remote(q.at[blk, 0:ATOMS], up.at[blk], up_send.at[blk], up_recv.at[blk], before)

    def low_copy(blk):
        return remote(
            cf.at[blk, ATOMS : 2 * ATOMS],
            cf.at[blk, 0:ATOMS],
            low_send.at[blk],
            low_recv.at[blk],
            after,
        )

    load_mix.wait()
    counts = meta[0:1, pl.ds(2 * SLOTS + start, WIN)].astype(F32)
    cw[64:72, :] = jnp.broadcast_to(counts, (8, WIN))
    prepare_tables(me, meta, cw, sel, b4, md, start)
    load_slots.wait()
    prepare_slots(pj, lf, lhs, bw)

    def project_block(blk):
        self_in(blk).wait()
        whole(xb.at[blk], in_recv.at[blk]).wait()
        split_bands(xb.at[blk], xs)
        project(slot_box, lhs, xs, pc, sel, q.at[blk])
        up_copy(blk).start()

    def couple_block(blk):
        up_copy(blk).wait_recv()
        couple(q.at[blk], up.at[blk], md, cf.at[blk])
        low_copy(blk).start()

    def apply_block(blk):
        low_copy(blk).wait_recv()
        contribute(me, slot_atom, cf.at[blk], k3, bw, cc)

        def ship(i, carry):
            peer = lax.rem(me + i, NSLAB)
            gather_boxes(peer, cc, b4, y.at[blk])
            remote(
                y.at[blk, peer],
                out.at[blk, rows_of(me), :],
                out_send.at[blk],
                out_recv.at[blk],
                peer,
            ).start()
            return carry

        lax.fori_loop(1, NSLAB, ship, 0)
        gather_boxes(me, cc, b4, y.at[blk])
        self_out(blk).start()

    project_block(0)
    couple_block(0)
    apply_block(0)
    project_block(1)
    couple_block(1)
    apply_block(1)

    for blk in range(2):
        whole(xb.at[blk], in_send.at[blk]).wait()
        up_copy(blk).wait_send()
        low_copy(blk).wait_send()
        self_out(blk).wait()
        whole(y.at[blk], out_send.at[blk]).wait()
        whole(y.at[blk], out_recv.at[blk]).wait()


def body(bands, projectors, slot_atom, slot_box, channels, coupling):
    nblock = bands.shape[0]
    ngrid = bands.shape[-1]
    meta = jnp.concatenate([slot_atom, slot_box, channels]).reshape(1, -1)
    any_space = pl.BlockSpec(memory_space=pl.ANY)
    smem = pl.BlockSpec(memory_space=pltpu.SMEM)
    vmem = pl.BlockSpec(memory_space=pltpu.VMEM)
    dma = pltpu.SemaphoreType.DMA
    result = pl.pallas_call(
        kernel,
        out_shape=jax.ShapeDtypeStruct((nblock, ngrid // 128, 128), F32),
        in_specs=[smem, smem, vmem, any_space, any_space, any_space],
        out_specs=any_space,
        scratch_shapes=[
            pltpu.VMEM((2, TILES, NB, 128), F32),
            pltpu.VMEM((BOXES, NB, 256), BF16),
            pltpu.VMEM((SLOTS, CH * PTS), F32),
            pltpu.VMEM((SLOTS * CH, 128), F32),
            pltpu.VMEM((SLOTS * CH, 256), BF16),
            pltpu.VMEM((HALF // 8, 128, 256), BF16),
            pltpu.VMEM((2 * ATOMS, SLOTS), BF16),
            pltpu.VMEM((4 * TILES, HALF), BF16),
            pltpu.VMEM((CH, ATOMS, CH * NB), F32),
            pltpu.VMEM((72, WIN), F32),
            pltpu.VMEM((CH * SLOTS, 128), F32),
            pltpu.VMEM((2, 2 * ATOMS, CH * NB), F32),
            pltpu.VMEM((2, ATOMS, CH * NB), F32),
            pltpu.VMEM((2, 2 * ATOMS, CH * NB), F32),
            pltpu.VMEM((2 * ATOMS, CH, 128), F32),
            pltpu.VMEM((HALF * NB, 128), F32),
            pltpu.VMEM((2, NSLAB, TILES, 128), F32),
            dma((2,)), dma((2,)), dma((2,)), dma((2,)),
            dma((2,)), dma((2,)), dma((2,)), dma((2,)),
            dma((2,)), dma((4,)),
        ],
        compiler_params=pltpu.CompilerParams(
            collective_id=0, has_side_effects=True, vmem_limit_bytes=60 * 1024 * 1024
        ),
        name="nonlocal",
    )(
        slot_atom,
        slot_box,
        meta,
        bands.reshape(nblock, ngrid // 128, 128),
        projectors,
        coupling.reshape(CH * CH, -1),
    )
    return result.reshape(bands.shape)


def solution(mesh):
    in_specs = (P(None, ("band", "slab"), None), P("slab", None), P("slab"), P("slab"), P(), P())
    out_specs = P(None, ("band", "slab"), None)
    return jax.shard_map(body, mesh=mesh, in_specs=in_specs, out_specs=out_specs, check_vma=False)
```

time: 375 us -> 104 us (0.28); the launches traced: 369 us -> 103 us
  local copies, waits for them, and re-layouts: 112 us -> 2.94 us
  matrix products: 106 us -> 0 us
  Pallas kernels: 0 us -> 99 us
  other arithmetic: 72 us -> 1.32 us
  waiting for transfers between devices: 32.7 us -> 0 us
  blocking collectives: 30.3 us -> 0 us
  starting transfers between devices: 14.9 us -> 0 us
    dot_general x5 -> x0, matrix products: 106 us -> none  [the longest x1 69.3 us: body(): jnp.einsum('nkbg,kcg->nkcb', patches, beta, precision=highest)]
    pallas_call x0 -> x1, Pallas kernels: none -> 99 us  [body(): pl.pallas_call(kernel, out_shape=jax.ShapeDtypeStruct((nblock, ngrid // 1...]
    scatter-add x1 -> x0, other arithmetic: 56.4 us -> none  [body(): summed = jnp.zeros((nitems, boxes, gathered_bands * BOXPTS), jnp.float32)...]
    reshape x12 -> x0, local copies, waits for them, and re-layouts: 38.2 us -> none  [the longest x1 13.4 us: body(): contrib = contrib.reshape(nitems, slots, gathered_bands * BOXPTS)]
    gather x2 -> x0, local copies, waits for them, and re-layouts: 32.5 us -> none  [body(): jnp.take(slab_grid, slot_box, axis=1)]
    all_to_all x1 -> x0, blocking collectives: 30.3 us -> none  [body(): lax.all_to_all(returning, 'slab', split_axis=1, concat_axis=2, tiled=True)]
    all_to_all x1 -> x0, waiting for transfers between devices: 22.9 us -> none  [body(): lax.all_to_all(arranged, 'slab', split_axis=2, concat_axis=1, tiled=True)]
    transpose x2 -> x0, local copies, waits for them, and re-layouts: 16.5 us -> none  [the longest x1 12.8 us: body(): contrib = jnp.einsum('nkcb,kcg->nkbg', per_slot, beta, precision=highest)]
  transfers between devices with their start and end apart: 3 -> 0, of which waited for: 3 -> 0; matrix products, arithmetic and copies ran while one was open for 2% -> 0% of each run, Pallas kernels for 0% -> 0%
where the time goes in v1:
time: 104 us; the launch traced here: 103 us
  Pallas kernels  99 us (95%)
  local copies, waits for them, and re-layouts  2.94 us (3%)
  other arithmetic  1.32 us (1%)
    pallas_call x1, Pallas kernels, body(): pl.pallas_call(kernel, out_shape=jax.ShapeDtypeStruct((nblock, ngrid // 1...  99 us
    unnamed x3, local copies, waits for them, and re-layouts  2.94 us

profile of v1, /device:TPU:8, one launch (start us, length us, event | category | flops | bytes accessed | tf_op | source)
XLA Modules:
  0.0 103.3 jit_solution(4846546644906869300)
XLA Ops:
  0.0 0.0 copy-start
  0.0 0.7 copy-done
  0.7 1.3 %pad_add_fusion = s32[4096]{0:T(1024)} fusion(s32[3072]{0:T(1024)} %param.10, s32[512]{0:T(512)} %slot_box.1, s32[512]{0:T(512)S(1)} %copy-done), kind=kLoop, calls=%fused_computation | loop fusion | flops 8192 | bytes 32768 | tf_op jit(solution)/shard_map/concatenate | solution.py:343
  2.0 99.0 %nonlocal.1 = f32[2,1024,128]{2,1,0:T(8,128)} custom-call(s32[512]{0:T(512)} %slot_atom.1, s32[512]{0:T(512)} %slot_box.1, s32[1,4096]{1,0:T(1,128)} %bitcast.7, f32[2,1024,128]{2,1,0:T(8,128)} %bitcast.5, f32[512,512]{1,0:T(8,128)} %projectors.1, f32[64,3072]{1,0:T(8,128)} %bitcast.6), custom_call_target="tpu_custom_call" | custom-call | tf_op jit(solution)/shard_map/nonlocal/pallas_call | solution.py:348
  101.0 2.3 %copy.9 = f32[2,1,131072]{2,1,0:T(1,128)} copy(f32[2,1,131072]{2,1,0:T(1,128)} %bitcast.4) | data formatting | bytes 2097152
Async XLA Ops:
  0.0 0.7 copy-start

commit v2 on v1

--- a/solution.py
+++ b/solution.py
@@ -18,6 +18,7 @@
 ATOMS = 96
 NATOM = NSLAB * ATOMS
 NB = 32
+STEP = 40
 WIN = 256
 
 
@@ -39,6 +40,19 @@
 
 def iota(shape, axis):
     return lax.broadcasted_iota(jnp.int32, shape, axis)
+
+
+def prepare_rows(me, slot_atom, rows_at):
+    prev_start = lax.rem(me + NSLAB - 1, NSLAB) * ATOMS
+
+    def one(k, carry):
+        atom = slot_atom[k]
+        rel = atom - prev_start
+        rel = jnp.where(rel < 0, rel + NATOM, rel)
+        rows_at[k] = jnp.where((atom < 0) | (rel >= 2 * ATOMS), 0, rel)
+        return carry
+
+    lax.fori_loop(0, SLOTS, one, 0, unroll=8)
 
 
 def prepare_slots(pj, lf, lhs, bw):
@@ -59,7 +73,7 @@
         lf[rows, :] = both
         return carry
 
-    lax.fori_loop(0, SLOTS * CH // 128, one, 0)
+    lax.fori_loop(0, SLOTS * CH // 128, one, 0, unroll=2)
     keep = (iota((16, 128), 0) < 8) == (iota((16, 128), 1) < 64)
 
     def two(g, carry):
@@ -126,7 +140,7 @@
             xs[2 * r + p, :, 128:256] = hi.astype(BF16)
         return carry
 
-    lax.fori_loop(0, TILES, one, 0, unroll=2)
+    lax.fori_loop(0, TILES, one, 0, unroll=8)
 
 
 def project(slot_box, lhs, xs, pc, sel, q):
@@ -142,7 +156,7 @@
             pc[pl.ds(base + i, CH, stride=SLOTS), :] = tile
         return carry
 
-    lax.fori_loop(0, SLOTS // 8, one, 0, unroll=4)
+    lax.fori_loop(0, SLOTS // 8, one, 0, unroll=16)
     values = jnp.concatenate(
         [pc[SLOTS * c : SLOTS * (c + 1), 0:NB] for c in range(CH)], axis=1
     )
@@ -158,27 +172,19 @@
     cf[ATOMS : 2 * ATOMS, :] = mixed
 
 
-def contribute(me, slot_atom, cf, k3, bw, cc):
+def contribute(rows_at, cf, k3, bw, cc):
     for c in range(CH):
         tile = cf[:, 128 * (c // 4) : 128 * (c // 4 + 1)]
         if c % 4:
             tile = pltpu.roll(tile, 128 - NB * (c % 4), 1)
         k3[:, c, :] = tile
-    prev_start = lax.rem(me + NSLAB - 1, NSLAB) * ATOMS
     pair_of = lax.div(lax.rem(iota((NB, WIN), 1), 128), 16)
-
-    def coefficients(k):
-        atom = slot_atom[k]
-        rel = atom - prev_start
-        rel = jnp.where(rel < 0, rel + NATOM, rel)
-        rel = jnp.where((atom < 0) | (rel >= 2 * ATOMS), 0, rel)
-        return k3[rel]
 
     def one(g, carry):
         parts = []
         for i in range(8):
-            parts.append(coefficients(g * 8 + i))
-            parts.append(coefficients(HALF + g * 8 + i))
+            parts.append(k3[rows_at[g * 8 + i]])
+            parts.append(k3[rows_at[HALF + g * 8 + i]])
         turned = jnp.transpose(jnp.concatenate(parts, axis=0))[0:NB, :]
         hi = turned.astype(BF16).astype(F32)
         lo = turned - hi
@@ -188,15 +194,18 @@
         )
         weights = bw[g]
         out = mm(rows, jnp.concatenate([weights, weights], axis=0))
-        cc[pl.ds(pl.multiple_of(g * 256, 256), 256), :] = out[:, 0:128] + out[:, 128:256]
-        return carry
-
-    lax.fori_loop(0, HALF // 8, one, 0, unroll=2)
+        out = out[:, 0:128] + out[:, 128:256]
+        for i in range(8):
+            first = pl.multiple_of((g * 8 + i) * STEP, 8)
+            cc[pl.ds(first, NB), :] = out[NB * i : NB * (i + 1), :]
+        return carry
+
+    lax.fori_loop(0, HALF // 8, one, 0, unroll=8)
 
 
 def gather_boxes(n, cc, b4, y):
     low = iota((TILES, 128), 1) < 64
-    hi, lo = split(cc[pl.ds(n, HALF, stride=NB), :])
+    hi, lo = split(cc[pl.ds(n, HALF, stride=STEP), :])
     out = mm(b4[...], jnp.concatenate([hi, lo], axis=1))
     out = out[:, 0:128] + out[:, 128:256]
     stay = jnp.where(low, out[0:32], out[96:128])
@@ -207,7 +216,7 @@
 def kernel(
     slot_atom, slot_box, meta, bands, projectors, coupling,
     out,
-    xb, xs, pj, lf, lhs, bw, sel, b4, md, cw, pc, q, up, cf, k3, cc, y,
+    xb, xs, pj, lf, lhs, bw, sel, b4, md, cw, pc, q, up, cf, k3, cc, y, rows_at,
     in_send, in_recv, out_send, out_recv, up_send, up_recv, low_send, low_recv, load_sem, self_sem,
 ):
     me = lax.axis_index("slab")
@@ -285,6 +294,7 @@
     load_mix.wait()
     counts = meta[0:1, pl.ds(2 * SLOTS + start, WIN)].astype(F32)
     cw[64:72, :] = jnp.broadcast_to(counts, (8, WIN))
+    prepare_rows(me, slot_atom, rows_at)
     prepare_tables(me, meta, cw, sel, b4, md, start)
     load_slots.wait()
     prepare_slots(pj, lf, lhs, bw)
@@ -303,11 +313,10 @@
 
     def apply_block(blk):
         low_copy(blk).wait_recv()
-        contribute(me, slot_atom, cf.at[blk], k3, bw, cc)
-
-        def ship(i, carry):
+        contribute(rows_at, cf.at[blk], k3, bw, cc)
+
+        def ship(i):
             peer = lax.rem(me + i, NSLAB)
-            gather_boxes(peer, cc, b4, y.at[blk])
             remote(
                 y.at[blk, peer],
                 out.at[blk, rows_of(me), :],
@@ -315,10 +324,19 @@
                 out_recv.at[blk],
                 peer,
             ).start()
+
+        def eight(g, carry):
+            for i in range(1, 9):
+                gather_boxes(lax.rem(me + g * 8 + i, NSLAB), cc, b4, y.at[blk])
+            for i in range(1, 9):
+                ship(g * 8 + i)
             return carry
 
-        lax.fori_loop(1, NSLAB, ship, 0)
-        gather_boxes(me, cc, b4, y.at[blk])
+        lax.fori_loop(0, 3, eight, 0)
+        for i in range(25, 33):
+            gather_boxes(lax.rem(me + i, NSLAB), cc, b4, y.at[blk])
+        for i in range(25, 32):
+            ship(i)
         self_out(blk).start()
 
     project_block(0)
@@ -366,8 +384,9 @@
             pltpu.VMEM((2, ATOMS, CH * NB), F32),
             pltpu.VMEM((2, 2 * ATOMS, CH * NB), F32),
             pltpu.VMEM((2 * ATOMS, CH, 128), F32),
-            pltpu.VMEM((HALF * NB, 128), F32),
+            pltpu.VMEM((HALF * STEP, 128), F32),
             pltpu.VMEM((2, NSLAB, TILES, 128), F32),
+            pltpu.SMEM((SLOTS,), jnp.int32),
             dma((2,)), dma((2,)), dma((2,)), dma((2,)),
             dma((2,)), dma((2,)), dma((2,)), dma((2,)),
             dma((2,)), dma((4,)),

time: 104 us -> 87.8 us (0.84)
  Pallas kernels: 99 us -> 82.1 us
    pallas_call x1, Pallas kernels: 99 us -> 82.1 us  [body(): pl.pallas_call(kernel, out_shape=jax.ShapeDtypeStruct((nblock, ngrid // 1...]
where the time goes in v2:
time: 87.8 us; the launch traced here: 86.4 us
  Pallas kernels  82.1 us (94%)
  local copies, waits for them, and re-layouts  2.94 us (3%)
  other arithmetic  1.32 us (2%)
    pallas_call x1, Pallas kernels, body(): pl.pallas_call(kernel, out_shape=jax.ShapeDtypeStruct((nblock, ngrid // 1...  82.1 us
    unnamed x3, local copies, waits for them, and re-layouts  2.94 us

profile of v2, /device:TPU:8, one launch (start us, length us, event | category | flops | bytes accessed | tf_op | source)
XLA Modules:
  0.0 86.4 jit_solution(12433045968934761161)
XLA Ops:
  0.0 0.0 copy-start
  0.0 0.7 copy-done
  0.7 1.3 %pad_add_fusion = s32[4096]{0:T(1024)} fusion(s32[3072]{0:T(1024)} %param.10, s32[512]{0:T(512)} %slot_box.1, s32[512]{0:T(512)S(1)} %copy-done), kind=kLoop, calls=%fused_computation | loop fusion | flops 8192 | bytes 32768 | tf_op jit(solution)/shard_map/concatenate | solution.py:361
  2.0 82.1 %nonlocal.1 = f32[2,1024,128]{2,1,0:T(8,128)} custom-call(s32[512]{0:T(512)} %slot_atom.1, s32[512]{0:T(512)} %slot_box.1, s32[1,4096]{1,0:T(1,128)} %bitcast.7, f32[2,1024,128]{2,1,0:T(8,128)} %bitcast.5, f32[512,512]{1,0:T(8,128)} %projectors.1, f32[64,3072]{1,0:T(8,128)} %bitcast.6), custom_call_target="tpu_custom_call" | custom-call | tf_op jit(solution)/shard_map/nonlocal/pallas_call | solution.py:366
  84.1 2.3 %copy.9 = f32[2,1,131072]{2,1,0:T(1,128)} copy(f32[2,1,131072]{2,1,0:T(1,128)} %bitcast.4) | data formatting | bytes 2097152
Async XLA Ops:
  0.0 0.7 copy-start

commit v3 on v2

--- a/solution.py
+++ b/solution.py
@@ -19,6 +19,9 @@
 NATOM = NSLAB * ATOMS
 NB = 32
 STEP = 40
+PARTS = 3
+EARLY = 22
+PART = ATOMS // PARTS
 WIN = 256
 
 
@@ -40,6 +43,15 @@
 
 def iota(shape, axis):
     return lax.broadcasted_iota(jnp.int32, shape, axis)
+
+
+def distance(i):
+    block = lax.div(i - 1, 2)
+    side = lax.rem(i - 1, 2)
+    far = lax.rem(block, 2)
+    step = lax.div(block, 2)
+    hops = (1 + step) * (1 - far) + (15 - step) * far
+    return hops * (1 - side) + (NSLAB - hops) * side
 
 
 def prepare_rows(me, slot_atom, rows_at):
@@ -91,9 +103,9 @@
     lax.fori_loop(0, HALF // 8, two, 0)
 
 
-def prepare_tables(me, meta, cw, sel, b4, md, start):
-    slot_atom = meta[0:1, 0:SLOTS]
-    slot_box = meta[0:1, SLOTS : 2 * SLOTS]
+def prepare_tables(me, atom_row, box_row, cw, sel, b4, md, start):
+    slot_atom = atom_row[...]
+    slot_box = box_row[...]
     live = slot_atom >= 0
     prev_start = lax.rem(me + NSLAB - 1, NSLAB) * ATOMS
     rel = slot_atom - prev_start
@@ -143,8 +155,8 @@
     lax.fori_loop(0, TILES, one, 0, unroll=8)
 
 
-def project(slot_box, lhs, xs, pc, sel, q):
-    def one(g, carry):
+def project(slot_box, lhs, xs, pc, sel, q, between):
+    def group(g):
         base = g * 8
         weights = jnp.concatenate([xs[slot_box[base + i]] for i in range(8)], axis=0)
         rows = pl.ds(pl.multiple_of(base * CH, 64), 64)
@@ -154,30 +166,45 @@
             if i % 4:
                 tile = pltpu.roll(tile, 128 - NB * (i % 4), 1)
             pc[pl.ds(base + i, CH, stride=SLOTS), :] = tile
-        return carry
-
-    lax.fori_loop(0, SLOTS // 8, one, 0, unroll=16)
+
+    def part(j, carry):
+        for i in range(16):
+            group(j * 16 + i)
+        return carry
+
+    lax.fori_loop(0, SLOTS // 128, part, 0)
     values = jnp.concatenate(
         [pc[SLOTS * c : SLOTS * (c + 1), 0:NB] for c in range(CH)], axis=1
     )
     hi, lo = split(values)
-    q[...] = mm(sel[...], hi) + mm(sel[...], lo)
-
-
-def couple(q, up, md, cf):
-    total = q[ATOMS : 2 * ATOMS, :] + up[...]
-    mixed = md[0] * total
+    for j in range(PARTS):
+        rows = slice(PART * j, PART * (j + 1))
+        q[rows, :] = mm(sel[rows, :], hi) + mm(sel[rows, :], lo)
+        between(j)
+    rows = slice(ATOMS, 2 * ATOMS)
+    q[rows, :] = mm(sel[rows, :], hi) + mm(sel[rows, :], lo)
+
+
+def couple(j, q, up, md, cf):
+    rows = slice(PART * j, PART * (j + 1))
+    own = slice(ATOMS + PART * j, ATOMS + PART * (j + 1))
+    total = q[own, :] + up[rows, :]
+    mixed = md[0, rows] * total
     for d in range(1, CH):
-        mixed = mixed + md[d] * pltpu.roll(total, NB * d, 1)
-    cf[ATOMS : 2 * ATOMS, :] = mixed
-
-
-def contribute(rows_at, cf, k3, bw, cc):
+        mixed = mixed + md[d, rows] * pltpu.roll(total, NB * d, 1)
+    cf[own, :] = mixed
+
+
+def spread_rows(first, cf, k3):
+    rows = slice(first, first + ATOMS)
     for c in range(CH):
-        tile = cf[:, 128 * (c // 4) : 128 * (c // 4 + 1)]
+        tile = cf[rows, 128 * (c // 4) : 128 * (c // 4 + 1)]
         if c % 4:
             tile = pltpu.roll(tile, 128 - NB * (c % 4), 1)
-        k3[:, c, :] = tile
+        k3[rows, c, :] = tile
+
+
+def contribute(rows_at, k3, bw, cc):
     pair_of = lax.div(lax.rem(iota((NB, WIN), 1), 128), 16)
 
     def one(g, carry):
@@ -214,21 +241,16 @@
 
 
 def kernel(
-    slot_atom, slot_box, meta, bands, projectors, coupling,
+    slot_atom, slot_box, channels, bands, projectors, coupling,
     out,
-    xb, xs, pj, lf, lhs, bw, sel, b4, md, cw, pc, q, up, cf, k3, cc, y, rows_at,
+    atom_row, box_row, count_row, atom_at, box_at, rows_at,
+    xb, xs, pj, lf, lhs, bw, sel, b4, md, cw, pc, q, up, cf, k3, cc, y,
     in_send, in_recv, out_send, out_recv, up_send, up_recv, low_send, low_recv, load_sem, self_sem,
 ):
     me = lax.axis_index("slab")
     after = lax.rem(me + 1, NSLAB)
     before = lax.rem(me + NSLAB - 1, NSLAB)
     start = pl.multiple_of(jnp.minimum(lax.div(me * ATOMS, 128) * 128, NATOM - WIN), 128)
-    load_slots = pltpu.make_async_copy(projectors, pj, load_sem.at[0])
-    load_slots.start()
-    load_mix = pltpu.make_async_copy(
-        coupling.at[:, pl.ds(start, WIN)], cw.at[0:64, :], load_sem.at[1]
-    )
-    load_mix.start()
 
     barrier = pltpu.get_barrier_semaphore()
 
@@ -239,6 +261,23 @@
         return carry
 
     lax.fori_loop(1, NSLAB, greet, 0)
+
+    loads = [
+        pltpu.make_async_copy(src, dst, load_sem.at[i])
+        for i, (src, dst) in enumerate(
+            [
+                (slot_atom, atom_row),
+                (slot_box, box_row),
+                (channels.at[:, pl.ds(start, WIN)], count_row),
+                (slot_atom.at[0], atom_at),
+                (slot_box.at[0], box_at),
+                (coupling.at[:, pl.ds(start, WIN)], cw.at[0:64, :]),
+                (projectors, pj),
+            ]
+        )
+    ]
+    for load in loads:
+        load.start()
     pl.semaphore_wait(barrier, NSLAB - 1)
 
     def rows_of(slab):
@@ -259,116 +298,132 @@
             src, dst, send_sem, recv_sem, device_id={"slab": peer}, device_id_type=MESH
         )
 
+    def send_in(blk, offset, batch):
+        peer = lax.rem(me + offset, NSLAB)
+        remote(
+            bands.at[blk, rows_of(peer), :],
+            xb.at[blk, :, me, :],
+            in_send.at[batch],
+            in_recv.at[blk],
+            peer,
+        ).start()
+
+    def send_out(blk, offset):
+        peer = lax.rem(me + offset, NSLAB)
+        remote(
+            y.at[blk, peer],
+            out.at[blk, rows_of(me), :],
+            out_send.at[blk],
+            out_recv.at[blk],
+            peer,
+        ).start()
+
+    def some(send, first, count):
+        def one(i, carry):
+            send(distance(first + i))
+            return carry
+
+        lax.fori_loop(0, count, one, 0)
+
+    def bytes_of(ref, count, sem):
+        part = ref.at[0:count]
+        return pltpu.make_async_copy(part, part, sem)
+
+    send_in(0, 16, 0)
+    some(lambda offset: send_in(0, offset, 0), 1, EARLY - 1)
+    some(lambda offset: send_in(0, offset, 1), EARLY, NSLAB - 1 - EARLY)
+    self_in(0).start()
+    self_in(1).start()
+
+    def up_copy(blk, j):
+        rows = slice(PART * j, PART * (j + 1))
+        return remote(
+            q.at[blk, rows], up.at[blk, rows], up_send.at[blk, j], up_recv.at[blk, j], before
+        )
+
+    def low_copy(blk, j):
+        return remote(
+            cf.at[blk, ATOMS + PART * j : ATOMS + PART * (j + 1)],
+            cf.at[blk, PART * j : PART * (j + 1)],
+            low_send.at[blk, j],
+            low_recv.at[blk, j],
+            after,
+        )
+
+    for load in loads:
+        load.wait()
+    prepare_slots(pj, lf, lhs, bw)
+    cw[64:72, :] = jnp.broadcast_to(count_row[...].astype(F32), (8, WIN))
+    prepare_tables(me, atom_row, box_row, cw, sel, b4, md, start)
+    prepare_rows(me, atom_at, rows_at)
+    bytes_of(xb.at[0], EARLY, in_send.at[0]).wait()
+    send_in(1, 16, 2)
+    some(lambda offset: send_in(1, offset, 2), 1, NSLAB - 2)
+
+    def gather(blk, offset):
+        gather_boxes(lax.rem(me + offset, NSLAB), cc, b4, y.at[blk])
+
+    def process(blk):
+        self_in(blk).wait()
+        bytes_of(xb.at[blk], NSLAB - 1, in_recv.at[blk]).wait()
+        split_bands(xb.at[blk], xs)
+        project(box_at, lhs, xs, pc, sel, q.at[blk], lambda j: up_copy(blk, j).start())
+        for j in range(PARTS):
+            up_copy(blk, j).wait_recv()
+            couple(j, q.at[blk], up.at[blk], md, cf.at[blk])
+            low_copy(blk, j).start()
+        spread_rows(ATOMS, cf.at[blk], k3)
+        for j in range(PARTS):
+            low_copy(blk, j).wait_recv()
+        spread_rows(0, cf.at[blk], k3)
+        contribute(rows_at, k3, bw, cc)
+
+        def eight(g, carry):
+            for i in range(8):
+                gather(blk, distance(1 + 8 * g + i))
+            some(lambda offset: send_out(blk, offset), 1 + 8 * g, 8)
+            return carry
+
+        lax.fori_loop(0, 3, eight, 0)
+        for i in range(25, 31):
+            gather(blk, distance(i))
+        gather(blk, 16)
+        gather(blk, 0)
+        some(lambda offset: send_out(blk, offset), 25, 6)
+        send_out(blk, 16)
+        self_out(blk).start()
+
+    process(0)
+    process(1)
+
+    bytes_of(xb.at[0], NSLAB - 1 - EARLY, in_send.at[1]).wait()
+    bytes_of(xb.at[1], NSLAB - 1, in_send.at[2]).wait()
     for blk in range(2):
-
-        def send(i, carry):
-            peer = lax.rem(me + i, NSLAB)
-            remote(
-                bands.at[blk, rows_of(peer), :],
-                xb.at[blk, :, me, :],
-                in_send.at[blk],
-                in_recv.at[blk],
-                peer,
-            ).start()
-            return carry
-
-        lax.fori_loop(1, NSLAB, send, 0)
-        self_in(blk).start()
-
-    def whole(ref, sem):
-        part = ref.at[0 : NSLAB - 1]
-        return pltpu.make_async_copy(part, part, sem)
-
-    def up_copy(blk):
-        return remote(q.at[blk, 0:ATOMS], up.at[blk], up_send.at[blk], up_recv.at[blk], before)
-
-    def low_copy(blk):
-        return remote(
-            cf.at[blk, ATOMS : 2 * ATOMS],
-            cf.at[blk, 0:ATOMS],
-            low_send.at[blk],
-            low_recv.at[blk],
-            after,
-        )
-
-    load_mix.wait()
-    counts = meta[0:1, pl.ds(2 * SLOTS + start, WIN)].astype(F32)
-    cw[64:72, :] = jnp.broadcast_to(counts, (8, WIN))
-    prepare_rows(me, slot_atom, rows_at)
-    prepare_tables(me, meta, cw, sel, b4, md, start)
-    load_slots.wait()
-    prepare_slots(pj, lf, lhs, bw)
-
-    def project_block(blk):
-        self_in(blk).wait()
-        whole(xb.at[blk], in_recv.at[blk]).wait()
-        split_bands(xb.at[blk], xs)
-        project(slot_box, lhs, xs, pc, sel, q.at[blk])
-        up_copy(blk).start()
-
-    def couple_block(blk):
-        up_copy(blk).wait_recv()
-        couple(q.at[blk], up.at[blk], md, cf.at[blk])
-        low_copy(blk).start()
-
-    def apply_block(blk):
-        low_copy(blk).wait_recv()
-        contribute(rows_at, cf.at[blk], k3, bw, cc)
-
-        def ship(i):
-            peer = lax.rem(me + i, NSLAB)
-            remote(
-                y.at[blk, peer],
-                out.at[blk, rows_of(me), :],
-                out_send.at[blk],
-                out_recv.at[blk],
-                peer,
-            ).start()
-
-        def eight(g, carry):
-            for i in range(1, 9):
-                gather_boxes(lax.rem(me + g * 8 + i, NSLAB), cc, b4, y.at[blk])
-            for i in range(1, 9):
-                ship(g * 8 + i)
-            return carry
-
-        lax.fori_loop(0, 3, eight, 0)
-        for i in range(25, 33):
-            gather_boxes(lax.rem(me + i, NSLAB), cc, b4, y.at[blk])
-        for i in range(25, 32):
-            ship(i)
-        self_out(blk).start()
-
-    project_block(0)
-    couple_block(0)
-    apply_block(0)
-    project_block(1)
-    couple_block(1)
-    apply_block(1)
-
-    for blk in range(2):
-        whole(xb.at[blk], in_send.at[blk]).wait()
-        up_copy(blk).wait_send()
-        low_copy(blk).wait_send()
+        for j in range(PARTS):
+            up_copy(blk, j).wait_send()
+            low_copy(blk, j).wait_send()
         self_out(blk).wait()
-        whole(y.at[blk], out_send.at[blk]).wait()
-        whole(y.at[blk], out_recv.at[blk]).wait()
+        bytes_of(y.at[blk], NSLAB - 1, out_send.at[blk]).wait()
+        bytes_of(y.at[blk], NSLAB - 1, out_recv.at[blk]).wait()
 
 
 def body(bands, projectors, slot_atom, slot_box, channels, coupling):
     nblock = bands.shape[0]
     ngrid = bands.shape[-1]
-    meta = jnp.concatenate([slot_atom, slot_box, channels]).reshape(1, -1)
     any_space = pl.BlockSpec(memory_space=pl.ANY)
-    smem = pl.BlockSpec(memory_space=pltpu.SMEM)
-    vmem = pl.BlockSpec(memory_space=pltpu.VMEM)
     dma = pltpu.SemaphoreType.DMA
     result = pl.pallas_call(
         kernel,
         out_shape=jax.ShapeDtypeStruct((nblock, ngrid // 128, 128), F32),
-        in_specs=[smem, smem, vmem, any_space, any_space, any_space],
+        in_specs=[any_space] * 6,
         out_specs=any_space,
         scratch_shapes=[
+            pltpu.VMEM((1, SLOTS), jnp.int32),
+            pltpu.VMEM((1, SLOTS), jnp.int32),
+            pltpu.VMEM((1, WIN), jnp.int32),
+            pltpu.SMEM((SLOTS,), jnp.int32),
+            pltpu.SMEM((SLOTS,), jnp.int32),
+            pltpu.SMEM((SLOTS,), jnp.int32),
             pltpu.VMEM((2, TILES, NB, 128), F32),
             pltpu.VMEM((BOXES, NB, 256), BF16),
             pltpu.VMEM((SLOTS, CH * PTS), F32),
@@ -386,19 +441,18 @@
             pltpu.VMEM((2 * ATOMS, CH, 128), F32),
             pltpu.VMEM((HALF * STEP, 128), F32),
             pltpu.VMEM((2, NSLAB, TILES, 128), F32),
-            pltpu.SMEM((SLOTS,), jnp.int32),
-            dma((2,)), dma((2,)), dma((2,)), dma((2,)),
-            dma((2,)), dma((2,)), dma((2,)), dma((2,)),
-            dma((2,)), dma((4,)),
+            dma((3,)), dma((2,)), dma((2,)), dma((2,)),
+            dma((2, PARTS)), dma((2, PARTS)), dma((2, PARTS)), dma((2, PARTS)),
+            dma((7,)), dma((4,)),
         ],
         compiler_params=pltpu.CompilerParams(
             collective_id=0, has_side_effects=True, vmem_limit_bytes=60 * 1024 * 1024
         ),
         name="nonlocal",
     )(
-        slot_atom,
-        slot_box,
-        meta,
+        slot_atom.reshape(1, -1),
+        slot_box.reshape(1, -1),
+        channels.reshape(1, -1),
         bands.reshape(nblock, ngrid // 128, 128),
         projectors,
         coupling.reshape(CH * CH, -1),

time: 87.8 us -> 82.7 us (0.942); the launches traced: 86.4 us -> 82.6 us
  Pallas kernels: 82.1 us -> 80.3 us
  other arithmetic: 1.32 us -> 0 us
    pallas_call x1, Pallas kernels: 82.1 us -> 80.3 us  [body(): pl.pallas_call(kernel, out_shape=jax.ShapeDtypeStruct((nblock, ngrid // 1...]
    concatenate x1 -> x0, other arithmetic: 1.32 us -> none  [body(): meta = jnp.concatenate([slot_atom, slot_box, channels]).reshape(1, -1)]
    unnamed x3 -> x1, local copies, waits for them, and re-layouts: 2.94 us -> 2.26 us
where the time goes in v3:
time: 82.7 us; the launch traced here: 82.6 us
  Pallas kernels  80.3 us (97%)
  local copies, waits for them, and re-layouts  2.26 us (3%)
    pallas_call x1, Pallas kernels, body(): pl.pallas_call(kernel, out_shape=jax.ShapeDtypeStruct((nblock, ngrid // 1...  80.3 us
    unnamed x1, local copies, waits for them, and re-layouts  2.26 us

profile of v3, /device:TPU:8, one launch (start us, length us, event | category | flops | bytes accessed | tf_op | source)
XLA Modules:
  0.0 82.6 jit_solution(10681211335820690834)
XLA Ops:
  0.0 80.3 %nonlocal.1 = f32[2,1024,128]{2,1,0:T(8,128)} custom-call(s32[1,512]{1,0:T(1,128)} %bitcast.10, s32[1,512]{1,0:T(1,128)} %bitcast.11, s32[1,3072]{1,0:T(1,128)} %bitcast.9, f32[2,1024,128]{2,1,0:T(8,128)} %bitcast.7, f32[512,512]{1,0:T(8,128)} %projectors.1, f32[64,3072]{1,0:T(8,128)} %bitcast.8), custom_call_target="tpu_custom_call" | custom-call | tf_op jit(solution)/shard_map/nonlocal/pallas_call | solution.py:415
  80.3 2.3 %copy.9 = f32[2,1,131072]{2,1,0:T(1,128)} copy(f32[2,1,131072]{2,1,0:T(1,128)} %bitcast.6) | data formatting | bytes 2097152

commit v4 on v3

--- a/solution.py
+++ b/solution.py
@@ -20,7 +20,7 @@
 NB = 32
 STEP = 40
 PARTS = 3
-EARLY = 22
+EARLY = 12
 PART = ATOMS // PARTS
 WIN = 256
 
@@ -177,12 +177,11 @@
         [pc[SLOTS * c : SLOTS * (c + 1), 0:NB] for c in range(CH)], axis=1
     )
     hi, lo = split(values)
-    for j in range(PARTS):
-        rows = slice(PART * j, PART * (j + 1))
+    for half in range(2):
+        rows = slice(ATOMS * half, ATOMS * (half + 1))
         q[rows, :] = mm(sel[rows, :], hi) + mm(sel[rows, :], lo)
-        between(j)
-    rows = slice(ATOMS, 2 * ATOMS)
-    q[rows, :] = mm(sel[rows, :], hi) + mm(sel[rows, :], lo)
+        if half == 0:
+            between()
 
 
 def couple(j, q, up, md, cf):
@@ -363,21 +362,30 @@
     def gather(blk, offset):
         gather_boxes(lax.rem(me + offset, NSLAB), cc, b4, y.at[blk])
 
-    def process(blk):
+    def project_block(blk):
+        def send_up():
+            for j in range(PARTS):
+                up_copy(blk, j).start()
+
         self_in(blk).wait()
         bytes_of(xb.at[blk], NSLAB - 1, in_recv.at[blk]).wait()
         split_bands(xb.at[blk], xs)
-        project(box_at, lhs, xs, pc, sel, q.at[blk], lambda j: up_copy(blk, j).start())
+        project(box_at, lhs, xs, pc, sel, q.at[blk], send_up)
+
+    def couple_block(blk):
         for j in range(PARTS):
             up_copy(blk, j).wait_recv()
             couple(j, q.at[blk], up.at[blk], md, cf.at[blk])
             low_copy(blk, j).start()
+
+    def contribute_block(blk):
         spread_rows(ATOMS, cf.at[blk], k3)
         for j in range(PARTS):
             low_copy(blk, j).wait_recv()
         spread_rows(0, cf.at[blk], k3)
         contribute(rows_at, k3, bw, cc)
 
+    def return_block(blk):
         def eight(g, carry):
             for i in range(8):
                 gather(blk, distance(1 + 8 * g + i))
@@ -393,8 +401,14 @@
         send_out(blk, 16)
         self_out(blk).start()
 
-    process(0)
-    process(1)
+    project_block(0)
+    couple_block(0)
+    project_block(1)
+    contribute_block(0)
+    couple_block(1)
+    return_block(0)
+    contribute_block(1)
+    return_block(1)
 
     bytes_of(xb.at[0], NSLAB - 1 - EARLY, in_send.at[1]).wait()
     bytes_of(xb.at[1], NSLAB - 1, in_send.at[2]).wait()

time: 82.7 us -> 73.4 us (0.89)
  Pallas kernels: 80.3 us -> 70.5 us
    pallas_call x1, Pallas kernels: 80.3 us -> 70.5 us  [body(): pl.pallas_call(kernel, out_shape=jax.ShapeDtypeStruct((nblock, ngrid // 1...]
where the time goes in v4:
time: 73.4 us; the launch traced here: 72.8 us
  Pallas kernels  70.5 us (96%)
  local copies, waits for them, and re-layouts  2.26 us (3%)
    pallas_call x1, Pallas kernels, body(): pl.pallas_call(kernel, out_shape=jax.ShapeDtypeStruct((nblock, ngrid // 1...  70.5 us
    unnamed x1, local copies, waits for them, and re-layouts  2.26 us

profile of v4, /device:TPU:8, one launch (start us, length us, event | category | flops | bytes accessed | tf_op | source)
XLA Modules:
  0.0 72.8 jit_solution(11790287183662738708)
XLA Ops:
  0.0 70.5 %nonlocal.1 = f32[2,1024,128]{2,1,0:T(8,128)} custom-call(s32[1,512]{1,0:T(1,128)} %bitcast.10, s32[1,512]{1,0:T(1,128)} %bitcast.11, s32[1,3072]{1,0:T(1,128)} %bitcast.9, f32[2,1024,128]{2,1,0:T(8,128)} %bitcast.7, f32[512,512]{1,0:T(8,128)} %projectors.1, f32[64,3072]{1,0:T(8,128)} %bitcast.8), custom_call_target="tpu_custom_call" | custom-call | tf_op jit(solution)/shard_map/nonlocal/pallas_call | solution.py:429
  70.5 2.3 %copy.9 = f32[2,1,131072]{2,1,0:T(1,128)} copy(f32[2,1,131072]{2,1,0:T(1,128)} %bitcast.6) | data formatting | bytes 2097152

commit v5 on v4

--- a/solution.py
+++ b/solution.py
@@ -20,7 +20,7 @@
 NB = 32
 STEP = 40
 PARTS = 3
-EARLY = 12
+PIECE = 16
 PART = ATOMS // PARTS
 WIN = 256
 
@@ -138,34 +138,38 @@
         )
 
 
-def split_bands(xb, xs):
-    low = iota((NB, 128), 1) < 64
+def split_bands(half, xb, xs):
+    low = iota((PIECE, 128), 1) < 64
+    bands = slice(PIECE * half, PIECE * (half + 1))
 
     def one(r, carry):
-        x = xb[r]
+        x = xb[r, bands, :]
         turned = pltpu.roll(x, 64, 1)
         for p in range(2):
             both = jnp.where(low, x, turned) if p == 0 else jnp.where(low, turned, x)
             hi = both.astype(BF16).astype(F32)
             lo = both - hi
-            xs[2 * r + p, :, 0:128] = jnp.where(low, hi, lo).astype(BF16)
-            xs[2 * r + p, :, 128:256] = hi.astype(BF16)
+            xs[2 * r + p, bands, 0:128] = jnp.where(low, hi, lo).astype(BF16)
+            xs[2 * r + p, bands, 128:256] = hi.astype(BF16)
         return carry
 
     lax.fori_loop(0, TILES, one, 0, unroll=8)
 
 
-def project(slot_box, lhs, xs, pc, sel, q, between):
+def project(half, slot_box, lhs, xs, pc):
+    lanes = slice(PIECE * half, PIECE * (half + 1))
+
     def group(g):
         base = g * 8
-        weights = jnp.concatenate([xs[slot_box[base + i]] for i in range(8)], axis=0)
+        weights = jnp.concatenate([xs[slot_box[base + i]][lanes, :] for i in range(8)], axis=0)
         rows = pl.ds(pl.multiple_of(base * CH, 64), 64)
         out = mm_nt(lhs[rows, :], weights)
         for i in range(8):
-            tile = out[8 * i : 8 * i + 8, 128 * (i // 4) : 128 * (i // 4 + 1)]
-            if i % 4:
-                tile = pltpu.roll(tile, 128 - NB * (i % 4), 1)
-            pc[pl.ds(base + i, CH, stride=SLOTS), :] = tile
+            tile = out[8 * i : 8 * i + 8, :]
+            if i != half:
+                tile = pltpu.roll(tile, (128 + PIECE * (half - i)) % 128, 1)
+            first = pl.multiple_of((base + i) * CH, CH)
+            pc[pl.ds(first, CH), lanes] = tile[:, lanes]
 
     def part(j, carry):
         for i in range(16):
@@ -173,14 +177,24 @@
         return carry
 
     lax.fori_loop(0, SLOTS // 128, part, 0)
+
+
+def collect(me, pc, sel, q, between):
     values = jnp.concatenate(
-        [pc[SLOTS * c : SLOTS * (c + 1), 0:NB] for c in range(CH)], axis=1
+        [pc[pl.ds(c, SLOTS, stride=CH), :][:, 0:NB] for c in range(CH)], axis=1
     )
     hi, lo = split(values)
-    for half in range(2):
-        rows = slice(ATOMS * half, ATOMS * (half + 1))
-        q[rows, :] = mm(sel[rows, :], hi) + mm(sel[rows, :], lo)
-        if half == 0:
+    shift = lax.rem(me + NSLAB - PIECE // 2, NSLAB)
+    inside = lax.rem(iota((ATOMS, 128), 1), NB) >= shift
+    for part in range(2):
+        rows = slice(ATOMS * part, ATOMS * (part + 1))
+        found = mm(sel[rows, :], hi) + mm(sel[rows, :], lo)
+        for t in range(2):
+            tile = found[:, 128 * t : 128 * (t + 1)]
+            ahead = pltpu.roll(tile, shift, 1)
+            behind = pltpu.roll(tile, lax.rem(shift + 96, 128), 1)
+            q[rows, 128 * t : 128 * (t + 1)] = jnp.where(inside, ahead, behind)
+        if part == 0:
             between()
 
 
@@ -226,7 +240,7 @@
             cc[pl.ds(first, NB), :] = out[NB * i : NB * (i + 1), :]
         return carry
 
-    lax.fori_loop(0, HALF // 8, one, 0, unroll=8)
+    lax.fori_loop(0, HALF // 8, one, 0, unroll=16)
 
 
 def gather_boxes(n, cc, b4, y):
@@ -284,7 +298,7 @@
 
     def self_in(blk):
         return pltpu.make_async_copy(
-            bands.at[blk, rows_of(me), :], xb.at[blk, :, me, :], self_sem.at[blk]
+            bands.at[blk, rows_of(me), :], xb.at[blk, :, PIECE // 2, :], self_sem.at[blk]
         )
 
     def self_out(blk):
@@ -297,15 +311,35 @@
             src, dst, send_sem, recv_sem, device_id={"slab": peer}, device_id_type=MESH
         )
 
-    def send_in(blk, offset, batch):
+    def send_in(blk, half, offset):
         peer = lax.rem(me + offset, NSLAB)
         remote(
             bands.at[blk, rows_of(peer), :],
-            xb.at[blk, :, me, :],
-            in_send.at[batch],
-            in_recv.at[blk],
+            xb.at[blk, :, lax.rem(NSLAB + PIECE // 2 - offset + NSLAB, NSLAB), :],
+            in_send.at[blk, half],
+            in_recv.at[blk, half],
             peer,
         ).start()
+
+    def send_near(blk):
+        def one(i, carry):
+            send_in(blk, 0, i)
+            send_in(blk, 0, NSLAB - i)
+            return carry
+
+        lax.fori_loop(1, 8, one, 0)
+        send_in(blk, 0, 8)
+
+    def send_far(blk):
+        send_in(blk, 1, 16)
+        send_in(blk, 1, 24)
+
+        def one(i, carry):
+            send_in(blk, 1, i)
+            send_in(blk, 1, NSLAB - i)
+            return carry
+
+        lax.fori_loop(9, 16, one, 0)
 
     def send_out(blk, offset):
         peer = lax.rem(me + offset, NSLAB)
@@ -328,9 +362,8 @@
         part = ref.at[0:count]
         return pltpu.make_async_copy(part, part, sem)
 
-    send_in(0, 16, 0)
-    some(lambda offset: send_in(0, offset, 0), 1, EARLY - 1)
-    some(lambda offset: send_in(0, offset, 1), EARLY, NSLAB - 1 - EARLY)
+    send_near(0)
+    send_far(0)
     self_in(0).start()
     self_in(1).start()
 
@@ -355,22 +388,28 @@
     cw[64:72, :] = jnp.broadcast_to(count_row[...].astype(F32), (8, WIN))
     prepare_tables(me, atom_row, box_row, cw, sel, b4, md, start)
     prepare_rows(me, atom_at, rows_at)
-    bytes_of(xb.at[0], EARLY, in_send.at[0]).wait()
-    send_in(1, 16, 2)
-    some(lambda offset: send_in(1, offset, 2), 1, NSLAB - 2)
+    send_near(1)
+    bytes_of(xb.at[0], PIECE - 1, in_send.at[0, 0]).wait()
+    send_far(1)
 
     def gather(blk, offset):
         gather_boxes(lax.rem(me + offset, NSLAB), cc, b4, y.at[blk])
 
-    def project_block(blk):
+    def project_near(blk):
+        self_in(blk).wait()
+        bytes_of(xb.at[blk], PIECE - 1, in_recv.at[blk, 0]).wait()
+        split_bands(0, xb.at[blk], xs)
+        project(0, box_at, lhs, xs, pc)
+
+    def project_far(blk):
         def send_up():
             for j in range(PARTS):
                 up_copy(blk, j).start()
 
-        self_in(blk).wait()
-        bytes_of(xb.at[blk], NSLAB - 1, in_recv.at[blk]).wait()
-        split_bands(xb.at[blk], xs)
-        project(box_at, lhs, xs, pc, sel, q.at[blk], send_up)
+        bytes_of(xb.at[blk], PIECE, in_recv.at[blk, 1]).wait()
+        split_bands(1, xb.at[blk], xs)
+        project(1, box_at, lhs, xs, pc)
+        collect(me, pc, sel, q.at[blk], send_up)
 
     def couple_block(blk):
         for j in range(PARTS):
@@ -401,17 +440,20 @@
         send_out(blk, 16)
         self_out(blk).start()
 
-    project_block(0)
+    project_near(0)
+    project_far(0)
+    project_near(1)
     couple_block(0)
-    project_block(1)
+    project_far(1)
     contribute_block(0)
     couple_block(1)
     return_block(0)
     contribute_block(1)
     return_block(1)
 
-    bytes_of(xb.at[0], NSLAB - 1 - EARLY, in_send.at[1]).wait()
-    bytes_of(xb.at[1], NSLAB - 1, in_send.at[2]).wait()
+    bytes_of(xb.at[0], PIECE, in_send.at[0, 1]).wait()
+    bytes_of(xb.at[1], PIECE - 1, in_send.at[1, 0]).wait()
+    bytes_of(xb.at[1], PIECE, in_send.at[1, 1]).wait()
     for blk in range(2):
         for j in range(PARTS):
             up_copy(blk, j).wait_send()
@@ -455,7 +497,7 @@
             pltpu.VMEM((2 * ATOMS, CH, 128), F32),
             pltpu.VMEM((HALF * STEP, 128), F32),
             pltpu.VMEM((2, NSLAB, TILES, 128), F32),
-            dma((3,)), dma((2,)), dma((2,)), dma((2,)),
+            dma((2, 2)), dma((2, 2)), dma((2,)), dma((2,)),
             dma((2, PARTS)), dma((2, PARTS)), dma((2, PARTS)), dma((2, PARTS)),
             dma((7,)), dma((4,)),
         ],

time: 73.4 us -> 71.1 us (0.969)
  Pallas kernels: 70.5 us -> 68.7 us
    pallas_call x1, Pallas kernels: 70.5 us -> 68.7 us  [body(): pl.pallas_call(kernel, out_shape=jax.ShapeDtypeStruct((nblock, ngrid // 1...]
where the time goes in v5:
time: 71.1 us; the launch traced here: 71 us
  Pallas kernels  68.7 us (97%)
  local copies, waits for them, and re-layouts  2.26 us (3%)
    pallas_call x1, Pallas kernels, body(): pl.pallas_call(kernel, out_shape=jax.ShapeDtypeStruct((nblock, ngrid // 1...  68.7 us
    unnamed x1, local copies, waits for them, and re-layouts  2.26 us

profile of v5, /device:TPU:8, one launch (start us, length us, event | category | flops | bytes accessed | tf_op | source)
XLA Modules:
  0.0 71.0 jit_solution(17211927968142483242)
XLA Ops:
  0.0 68.7 %nonlocal.1 = f32[2,1024,128]{2,1,0:T(8,128)} custom-call(s32[1,512]{1,0:T(1,128)} %bitcast.10, s32[1,512]{1,0:T(1,128)} %bitcast.11, s32[1,3072]{1,0:T(1,128)} %bitcast.9, f32[2,1024,128]{2,1,0:T(8,128)} %bitcast.7, f32[512,512]{1,0:T(8,128)} %projectors.1, f32[64,3072]{1,0:T(8,128)} %bitcast.8), custom_call_target="tpu_custom_call" | custom-call | tf_op jit(solution)/shard_map/nonlocal/pallas_call | solution.py:471
  68.7 2.3 %copy.9 = f32[2,1,131072]{2,1,0:T(1,128)} copy(f32[2,1,131072]{2,1,0:T(1,128)} %bitcast.6) | data formatting | bytes 2097152

commit v6 on v5

--- a/solution.py
+++ b/solution.py
@@ -19,7 +19,7 @@
 NATOM = NSLAB * ATOMS
 NB = 32
 STEP = 40
-PARTS = 3
+PARTS = 2
 PIECE = 16
 PART = ATOMS // PARTS
 WIN = 256
@@ -426,9 +426,10 @@
 
     def return_block(blk):
         def eight(g, carry):
-            for i in range(8):
-                gather(blk, distance(1 + 8 * g + i))
-            some(lambda offset: send_out(blk, offset), 1 + 8 * g, 8)
+            for j in range(2):
+                for i in range(4):
+                    gather(blk, distance(1 + 8 * g + 4 * j + i))
+                some(lambda offset: send_out(blk, offset), 1 + 8 * g + 4 * j, 4)
             return carry
 
         lax.fori_loop(0, 3, eight, 0)

time: 71.1 us -> 71.1 us (level)
  no operation moved by 1% of the time
where the time goes in v6:
time: 71.1 us; the launch traced here: 71 us
  Pallas kernels  68.7 us (97%)
  local copies, waits for them, and re-layouts  2.26 us (3%)
    pallas_call x1, Pallas kernels, body(): pl.pallas_call(kernel, out_shape=jax.ShapeDtypeStruct((nblock, ngrid // 1...  68.7 us
    unnamed x1, local copies, waits for them, and re-layouts  2.26 us

profile of v6, /device:TPU:8, one launch (start us, length us, event | category | flops | bytes accessed | tf_op | source)
XLA Modules:
  0.0 71.0 jit_solution(7520523637632957586)
XLA Ops:
  0.0 68.7 %nonlocal.1 = f32[2,1024,128]{2,1,0:T(8,128)} custom-call(s32[1,512]{1,0:T(1,128)} %bitcast.10, s32[1,512]{1,0:T(1,128)} %bitcast.11, s32[1,3072]{1,0:T(1,128)} %bitcast.9, f32[2,1024,128]{2,1,0:T(8,128)} %bitcast.7, f32[512,512]{1,0:T(8,128)} %projectors.1, f32[64,3072]{1,0:T(8,128)} %bitcast.8), custom_call_target="tpu_custom_call" | custom-call | tf_op jit(solution)/shard_map/nonlocal/pallas_call | solution.py:472
  68.7 2.3 %copy.9 = f32[2,1,131072]{2,1,0:T(1,128)} copy(f32[2,1,131072]{2,1,0:T(1,128)} %bitcast.6) | data formatting | bytes 2097152
